TPU v7x, 32 devices: a whole 2x2x4 slice. The times are simulated.
32 devices in a mesh: dp: 16 (over z, y, core), seq: 2 (over x).
Axes of the slice: x: 2, y: 2, z: 4, core: 2. Of those that a mesh axis runs over, the one named last changes fastest.
Arguments:
- hidden_in: bfloat16 [4096, 2048], P(('dp', 'seq')), may hold values from -6 to 6
- norm_gain: float32 [2048], replicated, may hold values from 0.5 to 1.5
- resid_grad: bfloat16 [4096, 2048], P(('dp', 'seq')), may hold values from -3 to 3
- key_output_gradient: bfloat16 [4096, 512], P('dp', 'seq'), may hold values from -6 to 6
- value_output_gradient: bfloat16 [4096, 512], P('dp', 'seq'), may hold values from -6 to 6
- key_matrix: bfloat16 [2048, 512], P(None, 'seq'), may hold values from -0.125 to 0.125
- value_matrix: bfloat16 [2048, 512], P(None, 'seq'), may hold values from -0.125 to 0.125
Outputs:
- input_grad: bfloat16 [4096, 2048], P(('dp', 'seq'))
- key_weight_grad: float32 [2048, 512], P('dp', 'seq')
- value_weight_grad: float32 [2048, 512], P('dp', 'seq')
- gain_grad: float32 [2048], replicated
All inputs are finite; a program needn't handle non-finite values.
Results may differ from a plain program's by a relative error of at most 0.0029.
Values may be sent and summed in bfloat16 or wider, within the bound.
No kernel may reach another device: no remote copies, remote signals or barrier semaphores. Data moves between devices by JAX's collectives and lax.ppermute only.
A program may use at most 64 MiB of HBM per device.

v0:
```python
import math
import jax
import jax.numpy as jnp
from jax import lax
from jax.sharding import PartitionSpec as P

EPSILON = 1e-05


def normalize(rows, norm_gain):
    widened = rows.astype(jnp.float32)
    inv_rms = lax.rsqrt(jnp.mean(widened * widened, axis=-1, keepdims=True) + EPSILON)
    unit_rows = widened * inv_rms
    return (inv_rms, unit_rows, (unit_rows * norm_gain).astype(jnp.bfloat16))


def per_device(
    hidden_in,
    norm_gain,
    resid_grad,
    key_output_gradient,
    value_output_gradient,
    key_matrix,
    value_matrix,
):
    model_width = hidden_in.shape[1]
    pair_width = key_matrix.shape[1]
    total_tokens = key_output_gradient.shape[0] * lax.axis_size("dp")
    scale = 1.0 / math.sqrt(total_tokens)
    inv_rms, unit_rows, normed = normalize(hidden_in, norm_gain)
    normed_piece = lax.all_gather(normed, "seq", axis=0, tiled=True)
    key_next = jnp.einsum(
        "td,tc->dc", normed_piece, key_output_gradient, preferred_element_type=jnp.float32
    )
    value_next = jnp.einsum(
        "td,tc->dc", normed_piece, value_output_gradient, preferred_element_type=jnp.float32
    )
    key_sum, value_sum = (
        lax.psum_scatter(key_next, "dp", scatter_dimension=0, tiled=True),
        lax.psum_scatter(value_next, "dp", scatter_dimension=0, tiled=True),
    )
    key_tok, value_tok = (
        lax.all_to_all(key_output_gradient, "seq", split_axis=0, concat_axis=1, tiled=True),
        lax.all_to_all(value_output_gradient, "seq", split_axis=0, concat_axis=1, tiled=True),
    )
    block_width = 2 * pair_width
    joined = jnp.concatenate([key_matrix, value_matrix], axis=1)
    piece = lax.all_gather(joined, "seq", axis=1, tiled=True)
    shards = piece.shape[1] // block_width
    blocks = piece.reshape(model_width, shards, block_width)
    key_piece = blocks[:, :, :pair_width].reshape(model_width, shards * pair_width)
    value_piece = blocks[:, :, pair_width:].reshape(model_width, shards * pair_width)
    key_term = jnp.einsum("tc,dc->td", key_tok, key_piece, preferred_element_type=jnp.float32)
    value_term = jnp.einsum("tc,dc->td", value_tok, value_piece, preferred_element_type=jnp.float32)
    normed_grad = key_term + value_term
    gain_total = lax.psum(jnp.sum(normed_grad * unit_rows, axis=0), ("dp", "seq"))
    scaled = normed_grad * norm_gain
    inner = jnp.mean(scaled * unit_rows, axis=-1, keepdims=True)
    input_grad = (resid_grad.astype(jnp.float32) + inv_rms * (scaled - unit_rows * inner)).astype(
        jnp.bfloat16
    )
    return (input_grad, key_sum * scale, value_sum * scale, gain_total * scale)


def solution(mesh):
    return jax.shard_map(
        per_device,
        mesh=mesh,
        in_specs=(
            P(("dp", "seq"), None),
            P(),
            P(("dp", "seq"), None),
            P("dp", "seq"),
            P("dp", "seq"),
            P(None, "seq"),
            P(None, "seq"),
        ),
        out_specs=(P(("dp", "seq"), None), P("dp", "seq"), P("dp", "seq"), P()),
        check_vma=False,
    )
```

profile of v0, /device:TPU:0, one launch (start us, length us, event | category | flops | bytes accessed | tf_op | source)
XLA Modules:
  0.0 237.8 jit_solution(16305939122774915193)
XLA Ops:
  7.2 1.5 copy.16
  8.7 1.5 copy.17
  10.2 1.4 pad_maximum_fusion
  11.7 4.4 %all-to-all-start.1 = ((bf16[2,128,256]{2,1,0:T(8,128)(2,1)}), bf16[2,128,256]{2,1,0:T(8,128)(2,1)S(1)}, u32[]{:S(2)}, u32[]{:S(2)}) async-start(bf16[2,128,256]{2,1,0:T(8,128)(2,1)} %bitcast.4), calls=%async_computation.1 | async-start | bytes 262144 | tf_op jit(solution)/shard_map/all_to_all | solution.py:44
  16.1 0.3 copy.15
  16.3 0.3 fusion.15
  16.6 4.0 %all-to-all-done.1 = bf16[2,128,256]{2,1,0:T(8,128)(2,1)S(1)} async-done(((bf16[2,128,256]{2,1,0:T(8,128)(2,1)}), bf16[2,128,256]{2,1,0:T(8,128)(2,1)S(1)}, u32[]{:S(2)}, u32[]{:S(2)}) %all-to-all-start.1) | async-done | bytes 131104 | tf_op jit(solution)/shard_map/all_to_all | solution.py:44
  20.6 3.4 %all-to-all-start = ((bf16[2,128,256]{2,1,0:T(8,128)(2,1)}), bf16[2,128,256]{2,1,0:T(8,128)(2,1)S(1)}, u32[]{:S(2)}, u32[]{:S(2)}) async-start(bf16[2,128,256]{2,1,0:T(8,128)(2,1)} %bitcast.1), calls=%async_computation | async-start | bytes 262144 | tf_op jit(solution)/shard_map/all_to_all | solution.py:43
  24.0 0.0 all-gather.5.cloned.1.call-start
  24.1 48.3 %all-gather.3.cloned.1.call-done = bf16[2048,1024]{0,1:T(8,128)(2,1)} async-done(((bf16[2048,512]{0,1:T(8,128)(2,1)}), bf16[2048,1024]{0,1:T(8,128)(2,1)}) %all-gather.3.cloned.1.call-update) | async-done | bytes 4194320 | tf_op jit(solution)/shard_map/all_gather | solution.py:48
  72.4 2.3 convolution_bitcast_fusion
  74.7 3.3 %fusion.14 = (f32[2048]{0:T(1024)S(1)}, f32[128]{0:T(128)S(1)}, bf16[128,2048]{0,1:T(8,128)(2,1)}, f32[128,2048]{0,1:T(8,128)S(1)}) fusion(bf16[128,2048]{0,1:T(8,128)(2,1)S(1)} %copy.15, f32[128]{0:T(128)S(1)} %add_rsqrt_fusion, f32[2048]{0:T(1024)S(1)} %copy-done.3, f32[2048,128]{1,0:T(8,128)S(1)} %convolution_bitcast_fusion, ...), kind=kOutput, calls=%fused_computation.19 | convolution fusion | flops 271054720 | bytes 5391360 | tf_op jit(solution)/shard_map/tc,dc->td/dot_general | solution.py:53
  78.1 21.7 %all-gather.5.cloned.1.call-done = bf16[256,2048]{0,1:T(8,128)(2,1)} async-done(((bf16[128,2048]{0,1:T(8,128)(2,1)}), bf16[256,2048]{0,1:T(8,128)(2,1)}) %all-gather.5.cloned.1.call-update) | async-done | bytes 1048592 | tf_op jit(solution)/shard_map/all_gather | solution.py:31
  99.8 3.1 %fusion.19 = f32[2048,256]{1,0:T(8,128)} fusion(bf16[256,2048]{0,1:T(8,128)(2,1)} %all-gather.5.cloned.1.call-done, bf16[256,256]{1,0:T(8,128)(2,1)} %param.11), kind=kOutput, calls=%fused_computation.29 | convolution fusion | flops 268435456 | bytes 3276800 | tf_op jit(solution)/shard_map/td,tc->dc/dot_general | solution.py:35
  102.9 2.7 %fusion.18 = f32[2048,256]{1,0:T(8,128)} fusion(bf16[256,2048]{0,1:T(8,128)(2,1)S(1)} %copy-done, bf16[256,256]{1,0:T(8,128)(2,1)} %param.10), kind=kOutput, calls=%fused_computation.28 | convolution fusion | flops 268435456 | bytes 3276800 | tf_op jit(solution)/shard_map/td,tc->dc/dot_general | solution.py:32
  105.7 0.3 copy.14
  106.0 0.4 fusion.12
  106.4 1.0 copy.20
  107.4 39.7 %psum.7 = f32[2048]{0:T(1024)S(1)} all-reduce(f32[2048]{0:T(1024)S(1)} %get-tuple-element.12), channel_id=1, replica_groups=mesh['dp'=16,'seq'=2] {'dp','seq'}, use_global_device_ids=true, to_apply=%region_5.0 | all-reduce | flops 2048 | bytes 16384 | tf_op jit(solution)/shard_map/psum | solution.py:56
  147.1 0.6 broadcast_multiply_fusion.2
  147.7 17.6 %reduce-scatter.5.cloned.1.call-done = f32[128,256]{1,0:T(8,128)} async-done(((f32[2048,256]{1,0:T(8,128)}), f32[128,256]{1,0:T(8,128)}) %reduce-scatter.5.cloned.1.call-update) | async-done | bytes 131088 | tf_op jit(solution)/shard_map/reduce_scatter | solution.py:40
  165.3 1.6 broadcast_multiply_fusion
  166.9 62.8 %reduce-scatter.3.cloned.1.call-done = f32[128,256]{1,0:T(8,128)} async-done(((f32[2048,256]{1,0:T(8,128)}), f32[128,256]{1,0:T(8,128)}) %reduce-scatter.3.cloned.1.call-update) | async-done | bytes 131088 | tf_op jit(solution)/shard_map/reduce_scatter | solution.py:39
  229.7 1.6 broadcast_multiply_fusion.1
  (18 shorter events, 0.2 us)
Async XLA Ops:
  7.2 65.2 %all-gather.3.cloned.1.call-start = ((), (), s32[]{:S(2)}) async-start(), calls=%async_computation.4 | async-start | bytes 6291456 | tf_op jit(solution)/shard_map/all_gather | solution.py:48
  11.6 4.4 %copy-start.1 = (bf16[128,2048]{1,0:T(8,128)(2,1)S(1)}, bf16[128,2048]{1,0:T(8,128)(2,1)}, u32[]{:S(2)}) copy-start(bf16[128,2048]{1,0:T(8,128)(2,1)} %param.7) | copy-start | bytes 1572868
  11.7 8.9 %all-to-all-start.1 = ((bf16[2,128,256]{2,1,0:T(8,128)(2,1)}), bf16[2,128,256]{2,1,0:T(8,128)(2,1)S(1)}, u32[]{:S(2)}, u32[]{:S(2)}) async-start(bf16[2,128,256]{2,1,0:T(8,128)(2,1)} %bitcast.4), calls=%async_computation.1 | async-start | bytes 262144 | tf_op jit(solution)/shard_map/all_to_all | solution.py:44
  16.3 58.4 %copy-start.3 = (f32[2048]{0:T(1024)S(1)}, f32[2048]{0:T(1024)}, u32[]{:S(2)}) copy-start(f32[2048]{0:T(1024)} %param.8) | copy-start | bytes 24580
  20.6 54.1 %all-to-all-start = ((bf16[2,128,256]{2,1,0:T(8,128)(2,1)}), bf16[2,128,256]{2,1,0:T(8,128)(2,1)S(1)}, u32[]{:S(2)}, u32[]{:S(2)}) async-start(bf16[2,128,256]{2,1,0:T(8,128)(2,1)} %bitcast.1), calls=%async_computation | async-start | bytes 262144 | tf_op jit(solution)/shard_map/all_to_all | solution.py:43
  24.0 75.7 %all-gather.5.cloned.1.call-start = ((), (), s32[]{:S(2)}) async-start(), calls=%async_computation.5 | async-start | bytes 1572864 | tf_op jit(solution)/shard_map/all_gather | solution.py:31
  78.0 87.3 %reduce-scatter.5.cloned.1.call-start = ((), (), s32[]{:S(2)}) async-start(), calls=%async_computation.7 | async-start | bytes 2228224 | tf_op jit(solution)/shard_map/reduce_scatter | solution.py:40
  99.8 3.2 %copy-start = (bf16[256,2048]{0,1:T(8,128)(2,1)S(1)}, bf16[256,2048]{0,1:T(8,128)(2,1)}, u32[]{:S(2)}) copy-start(bf16[256,2048]{0,1:T(8,128)(2,1)} %all-gather.5.cloned.1.call-done) | copy-start | bytes 3145732
  102.9 2.8 %copy-start.2 = (bf16[128,2048]{1,0:T(8,128)(2,1)S(1)}, bf16[128,2048]{1,0:T(8,128)(2,1)}, u32[]{:S(2)}) copy-start(bf16[128,2048]{1,0:T(8,128)(2,1)} %param.9) | copy-start | bytes 1572868
  102.9 126.8 %reduce-scatter.3.cloned.1.call-start = ((), (), s32[]{:S(2)}) async-start(), calls=%async_computation.6 | async-start | bytes 2228224 | tf_op jit(solution)/shard_map/reduce_scatter | solution.py:39
Sparse Core Ops, SparseCore 0:
  11.8 60.5 all-gather.2
  78.2 21.5 all-gather.4
  103.5 61.7 reduce-scatter.4
  168.9 60.7 reduce-scatter.2
where the time goes:
time: 238 us
  waiting for transfers between devices  154 us (65%)
  blocking collectives  39.7 us (17%)
  between operations  13.9 us (6%)
  matrix products  11.4 us (5%)
  starting transfers between devices  7.94 us (3%)
  other arithmetic  5.9 us (2%)
  local copies, waits for them, and re-layouts  4.55 us (2%)
    reduce_scatter x1, waiting for transfers between devices, per_device(): lax.psum_scatter(key_next, 'dp', scatter_dimension=0, tiled=True)  62.8 us
    all_gather x1, waiting for transfers between devices, per_device(): piece = lax.all_gather(joined, 'seq', axis=1, tiled=True)  48.3 us
    psum x1, blocking collectives, per_device(): lax.psum(jnp.sum(normed_grad * unit_rows, axis=0), ('dp', 'seq'))  39.7 us
    all_gather x1, waiting for transfers between devices, per_device(): normed_piece = lax.all_gather(normed, 'seq', axis=0, tiled=True)  21.7 us
    reduce_scatter x1, waiting for transfers between devices, per_device(): lax.psum_scatter(value_next, 'dp', scatter_dimension=0, tiled=True)  17.6 us
  transfers between devices with their start and end apart: 6, of which 5 were waited for; matrix products, arithmetic and copies ran while one was open for 4% of the time, Pallas kernels for 0%

commit v1 on v0

--- a/solution.py
+++ b/solution.py
@@ -28,7 +28,15 @@
     total_tokens = key_output_gradient.shape[0] * lax.axis_size("dp")
     scale = 1.0 / math.sqrt(total_tokens)
     inv_rms, unit_rows, normed = normalize(hidden_in, norm_gain)
-    normed_piece = lax.all_gather(normed, "seq", axis=0, tiled=True)
+    ways, here = (lax.axis_size("seq"), lax.axis_index("seq"))
+    grown, reach = (normed, 1)
+    while reach < ways:
+        theirs = lax.ppermute(grown, "seq", [(d, d ^ reach) for d in range(ways)])
+        mine_first = jnp.concatenate([grown, theirs], axis=0)
+        theirs_first = jnp.concatenate([theirs, grown], axis=0)
+        grown = jnp.where(here & reach == 0, mine_first, theirs_first)
+        reach = 2 * reach
+    normed_piece = grown
     key_next = jnp.einsum(
         "td,tc->dc", normed_piece, key_output_gradient, preferred_element_type=jnp.float32
     )

time: 238 us -> 230 us (0.966)
  waiting for transfers between devices: 154 us -> 145 us
    all_gather x1 -> x0, waiting for transfers between devices: 21.7 us -> none  [per_device(): normed_piece = lax.all_gather(normed, 'seq', axis=0, tiled=True)]
    ppermute x0 -> x1, waiting for transfers between devices: none -> 13.4 us  [per_device(): theirs = lax.ppermute(grown, 'seq', [(d, d ^ reach) for d in range(ways)])]
  transfers between devices with their start and end apart: 6 -> 6, of which waited for: 5 -> 5; matrix products, arithmetic and copies ran while one was open for 4% -> 5% of each run, Pallas kernels for 0% -> 0%
where the time goes in v1:
time: 230 us; the launch traced here: 229 us
  waiting for transfers between devices  145 us (63%)
  blocking collectives  40.1 us (17%)
  between operations  13.8 us (6%)
  matrix products  11.7 us (5%)
  starting transfers between devices  8.25 us (4%)
  other arithmetic  5.91 us (3%)
  local copies, waits for them, and re-layouts  4.79 us (2%)
    reduce_scatter x1, waiting for transfers between devices, per_device(): lax.psum_scatter(key_next, 'dp', scatter_dimension=0, tiled=True)  62.9 us
    all_gather x1, waiting for transfers between devices, per_device(): piece = lax.all_gather(joined, 'seq', axis=1, tiled=True)  48.3 us
    psum x1, blocking collectives, per_device(): lax.psum(jnp.sum(normed_grad * unit_rows, axis=0), ('dp', 'seq'))  40.1 us
    reduce_scatter x1, waiting for transfers between devices, per_device(): lax.psum_scatter(value_next, 'dp', scatter_dimension=0, tiled=True)  16.2 us
    ppermute x1, waiting for transfers between devices, per_device(): theirs = lax.ppermute(grown, 'seq', [(d, d ^ reach) for d in range(ways)])  13.4 us
    unnamed x13, local copies, waits for them, and re-layouts  4.79 us
  transfers between devices with their start and end apart: 6, of which 5 were waited for; matrix products, arithmetic and copies ran while one was open for 5% of the time, Pallas kernels for 0%

profile of v1, /device:TPU:0, one launch (start us, length us, event | category | flops | bytes accessed | tf_op | source)
XLA Modules:
  0.0 229.4 jit_solution(10486366977643657375)
XLA Ops:
  7.2 1.6 copy.16
  8.8 0.6 copy.17
  9.5 1.5 pad_maximum_fusion
  10.9 4.4 %all-to-all-start.1 = ((bf16[2,128,256]{2,1,0:T(8,128)(2,1)}), bf16[2,128,256]{2,1,0:T(8,128)(2,1)S(1)}, u32[]{:S(2)}, u32[]{:S(2)}) async-start(bf16[2,128,256]{2,1,0:T(8,128)(2,1)} %bitcast.4), calls=%async_computation.1 | async-start | bytes 262144 | tf_op jit(solution)/shard_map/all_to_all | solution.py:52
  15.3 0.3 copy.15
  15.6 0.3 fusion.15
  15.9 4.0 %all-to-all-done.1 = bf16[2,128,256]{2,1,0:T(8,128)(2,1)S(1)} async-done(((bf16[2,128,256]{2,1,0:T(8,128)(2,1)}), bf16[2,128,256]{2,1,0:T(8,128)(2,1)S(1)}, u32[]{:S(2)}, u32[]{:S(2)}) %all-to-all-start.1) | async-done | bytes 131104 | tf_op jit(solution)/shard_map/all_to_all | solution.py:52
  19.9 3.4 %all-to-all-start = ((bf16[2,128,256]{2,1,0:T(8,128)(2,1)}), bf16[2,128,256]{2,1,0:T(8,128)(2,1)S(1)}, u32[]{:S(2)}, u32[]{:S(2)}) async-start(bf16[2,128,256]{2,1,0:T(8,128)(2,1)} %bitcast.1), calls=%async_computation | async-start | bytes 262144 | tf_op jit(solution)/shard_map/all_to_all | solution.py:51
  23.3 48.3 %all-gather.2.cloned.1.call-done = bf16[2048,1024]{0,1:T(8,128)(2,1)} async-done(((bf16[2048,512]{0,1:T(8,128)(2,1)}), bf16[2048,1024]{0,1:T(8,128)(2,1)}) %all-gather.2.cloned.1.call-update) | async-done | bytes 4194320 | tf_op jit(solution)/shard_map/all_gather | solution.py:56
  71.6 3.3 %convolution_bitcast_fusion = f32[2048,128]{1,0:T(8,128)} fusion(bf16[2048,2,512]{0,2,1:T(8,128)(2,1)} %bitcast.23, bf16[2,128,256]{2,1,0:T(8,128)(2,1)S(1)} %all-to-all-done.1), kind=kOutput, calls=%fused_computation | convolution fusion | flops 268435456 | bytes 3276800 | tf_op jit(solution)/shard_map/tc,dc->td/dot_general | solution.py:62
  74.9 3.1 %fusion.14 = (f32[2048]{0:T(1024)S(1)}, f32[128]{0:T(128)S(1)}, bf16[128,2048]{0,1:T(8,128)(2,1)S(1)}, f32[128,2048]{0,1:T(8,128)S(1)}) fusion(bf16[128,2048]{0,1:T(8,128)(2,1)S(1)} %copy.15, f32[128]{0:T(128)S(1)} %add_rsqrt_fusion, f32[2048]{0:T(1024)S(1)} %copy-done.3, f32[2048,128]{1,0:T(8,128)} %convolution_bitcast_fusion, ...), kind=kOutput, calls=%fused_computation.19 | convolution fusion | flops 271054720 | bytes 5391360 | tf_op jit(solution)/shard_map/tc,dc->td/dot_general | solution.py:61
  78.0 0.4 collective-permute-start
  78.3 13.4 %collective-permute-done = bf16[128,2048]{0,1:T(8,128)(2,1)S(1)} collective-permute-done((bf16[128,2048]{0,1:T(8,128)(2,1)S(1)}, bf16[128,2048]{0,1:T(8,128)(2,1)S(1)}, u32[]{:S(2)}, u32[]{:S(2)}) %collective-permute-start) | collective-permute-done | bytes 524320 | tf_op jit(solution)/shard_map/ppermute | solution.py:34
  91.8 2.6 %fusion.16 = f32[2048,256]{1,0:T(8,128)} fusion(bf16[256,256]{1,0:T(8,128)(2,1)} %param.11, bf16[128,2048]{0,1:T(8,128)(2,1)S(1)} %collective-permute-done, bf16[128,2048]{0,1:T(8,128)(2,1)S(1)} %get-tuple-element.14, pred[]{:T(512)S(6)} %eq.3), kind=kOutput, calls=%fused_computation.22 | convolution fusion | flops 273154048 | bytes 3276801 | tf_op jit(solution)/shard_map/td,tc->dc/dot_general | solution.py:43
  94.5 2.7 %fusion.17 = f32[2048,256]{1,0:T(8,128)} fusion(bf16[256,256]{1,0:T(8,128)(2,1)} %param.10, bf16[128,2048]{0,1:T(8,128)(2,1)S(1)} %collective-permute-done, bf16[128,2048]{0,1:T(8,128)(2,1)S(1)} %get-tuple-element.14, pred[]{:T(512)S(6)} %eq.3), kind=kOutput, calls=%fused_computation.23 | convolution fusion | flops 273154048 | bytes 3276801 | tf_op jit(solution)/shard_map/td,tc->dc/dot_general | solution.py:40
  97.2 1.0 copy-done.2
  98.5 0.4 fusion.12
  98.9 1.0 copy.20
  100.0 40.1 %psum.7 = f32[2048]{0:T(1024)S(1)} all-reduce(f32[2048]{0:T(1024)S(1)} %get-tuple-element.12), channel_id=1, replica_groups=mesh['dp'=16,'seq'=2] {'dp','seq'}, use_global_device_ids=true, to_apply=%region_5.6 | all-reduce | flops 2048 | bytes 16384 | tf_op jit(solution)/shard_map/psum | solution.py:64
  140.0 0.6 broadcast_multiply_fusion.2
  140.6 16.2 %reduce-scatter.5.cloned.1.call-done = f32[128,256]{1,0:T(8,128)} async-done(((f32[2048,256]{1,0:T(8,128)}), f32[128,256]{1,0:T(8,128)}) %reduce-scatter.5.cloned.1.call-update) | async-done | bytes 131088 | tf_op jit(solution)/shard_map/reduce_scatter | solution.py:48
  156.8 1.6 broadcast_multiply_fusion
  158.4 62.9 %reduce-scatter.3.cloned.1.call-done = f32[128,256]{1,0:T(8,128)} async-done(((f32[2048,256]{1,0:T(8,128)}), f32[128,256]{1,0:T(8,128)}) %reduce-scatter.3.cloned.1.call-update) | async-done | bytes 131088 | tf_op jit(solution)/shard_map/reduce_scatter | solution.py:47
  221.3 1.6 broadcast_multiply_fusion.1
  (17 shorter events, 0.5 us)
Async XLA Ops:
  7.2 1.6 copy-start
  7.2 64.4 %all-gather.2.cloned.1.call-start = ((), (), s32[]{:S(2)}) async-start(), calls=%async_computation.4 | async-start | bytes 6291456 | tf_op jit(solution)/shard_map/all_gather | solution.py:56
  10.9 4.4 %copy-start.1 = (bf16[128,2048]{1,0:T(8,128)(2,1)S(1)}, bf16[128,2048]{1,0:T(8,128)(2,1)}, u32[]{:S(2)}) copy-start(bf16[128,2048]{1,0:T(8,128)(2,1)} %param.7) | copy-start | bytes 1572868
  10.9 8.9 %all-to-all-start.1 = ((bf16[2,128,256]{2,1,0:T(8,128)(2,1)}), bf16[2,128,256]{2,1,0:T(8,128)(2,1)S(1)}, u32[]{:S(2)}, u32[]{:S(2)}) async-start(bf16[2,128,256]{2,1,0:T(8,128)(2,1)} %bitcast.4), calls=%async_computation.1 | async-start | bytes 262144 | tf_op jit(solution)/shard_map/all_to_all | solution.py:52
  15.6 59.3 %copy-start.3 = (f32[2048]{0:T(1024)S(1)}, f32[2048]{0:T(1024)}, u32[]{:S(2)}) copy-start(f32[2048]{0:T(1024)} %param.8) | copy-start | bytes 24580
  19.9 55.0 %all-to-all-start = ((bf16[2,128,256]{2,1,0:T(8,128)(2,1)}), bf16[2,128,256]{2,1,0:T(8,128)(2,1)S(1)}, u32[]{:S(2)}, u32[]{:S(2)}) async-start(bf16[2,128,256]{2,1,0:T(8,128)(2,1)} %bitcast.1), calls=%async_computation | async-start | bytes 262144 | tf_op jit(solution)/shard_map/all_to_all | solution.py:51
  23.3 133.5 %reduce-scatter.5.cloned.1.call-start = ((), (), s32[]{:S(2)}) async-start(), calls=%async_computation.6 | async-start | bytes 2228224 | tf_op jit(solution)/shard_map/reduce_scatter | solution.py:48
  78.0 13.8 %collective-permute-start = (bf16[128,2048]{0,1:T(8,128)(2,1)S(1)}, bf16[128,2048]{0,1:T(8,128)(2,1)S(1)}, u32[]{:S(2)}, u32[]{:S(2)}) collective-permute-start(bf16[128,2048]{0,1:T(8,128)(2,1)S(1)} %get-tuple-element.14), channel_id=1, source_target_pairs={{0,1},{1,0},{2,3},{3,2},{4,5},{5,4},{6,7},{7,6},{8,9},{9,8},{10,11... | collective-permute-start | bytes 1572872 | tf_op jit(solution)/shard_map/ppermute | solution.py:34
  94.4 126.8 %reduce-scatter.3.cloned.1.call-start = ((), (), s32[]{:S(2)}) async-start(), calls=%async_computation.5 | async-start | bytes 2228224 | tf_op jit(solution)/shard_map/reduce_scatter | solution.py:47
  97.2 1.0 copy-start.2
Sparse Core Ops, SparseCore 0:
  11.1 60.5 all-gather.1
  94.6 62.1 reduce-scatter.4
  160.5 60.6 reduce-scatter.2
